TPU v7x, 32 devices: a whole 2x2x4 slice. The times are simulated.
32 devices in a mesh: grp: 2 (over y), keys: 4 (over x, core), qry: 4 (over z).
Axes of the slice: x: 2, y: 2, z: 4, core: 2. Of those that a mesh axis runs over, the one named last changes fastest.
Arguments:
- queries: bfloat16 [4096, 8, 128], P(('grp', 'keys', 'qry')), parts along dimension 0, may hold values from -40 to 40, as said below
- cache_keys: bfloat16 [4096, 128], P(('grp', 'keys')), parts along dimension 0, may hold values from -128 to 128, as said below
- cache_values: bfloat16 [4096, 128], P(('grp', 'keys')), parts along dimension 0, may hold values from -24 to 24
- entry: int32 [8, 4], P(('grp', 'keys'), 'qry'), parts along dimension 0, may hold values from 0 to 3
- visits: int32 [8, 4], P(('grp', 'keys'), 'qry'), parts along dimension 0, may hold values from 3 to 4
- doc_length: int32 [2], P('grp'), parts along dimension 0, may hold values from 1025 to 2048
- slot_params: float32 [2048, 256], P(('grp', 'keys', 'qry')), parts along dimension 0, may hold values from -128 to 128, as said below
- first_moment: float32 [2048, 256], P(('grp', 'keys', 'qry')), parts along dimension 0, may hold values from -3 to 3
- second_moment: float32 [2048, 256], P(('grp', 'keys', 'qry')), parts along dimension 0, may hold values from 0.05 to 1
Outputs:
- teacher_out: bfloat16 [4096, 8, 128], P(('grp', 'keys', 'qry')), parts along dimension 0
- slot_grad: float32 [2048, 256], P(('grp', 'keys', 'qry')), parts along dimension 0
- new_params: float32 [2048, 256], P(('grp', 'keys', 'qry')), parts along dimension 0
- new_first: float32 [2048, 256], P(('grp', 'keys', 'qry')), parts along dimension 0
- new_second: float32 [2048, 256], P(('grp', 'keys', 'qry')), parts along dimension 0
- loss: float32 [2], P('grp'), parts along dimension 0
There are 2 independent parts, one for each index of `grp`. A program takes and returns all parts, laid end to end along the dimension named above; each array names one. Nothing has to cross between parts.
Inputs may be any that keep to these rules, and one draw needn't show every extreme that they name: `queries`: query entries stay within the stated range. `cache_keys`: cache key entries stay within the stated range. `slot_params`: slot entries stay within the stated range.
All inputs are finite; a program needn't handle non-finite values.
Results may differ from a plain program's by a relative error of at most 0.0045.
Values may be sent and summed in bfloat16 or wider, within the bound.
No kernel may reach another device: no remote copies, remote signals or barrier semaphores. Data moves between devices by JAX's collectives and lax.ppermute only.
A program may use at most 64 MiB of HBM per device.

v0:
```python
import math
import jax
import jax.numpy as jnp
from jax import lax
from jax.sharding import PartitionSpec as P

NEG = -1e30


def shifted(block, axis, distance):
    devices = range(lax.axis_size(axis))
    route = [((i - distance) % len(devices), i) for i in devices]
    return lax.ppermute(block, axis, route)


def row_scores(left, right):
    return lax.dot_general(
        left, right, (((1,), (1,)), ((), ())), preferred_element_type=jnp.float32
    )


def attend(state, query_blocks, keys, values, shard, length, score_scale):
    block_width = keys.shape[0]
    place = shard * block_width + lax.iota(jnp.int32, block_width)
    live = (place < length)[None, :]

    def one(block_entry):
        query_portion, big, total, acc = block_entry
        logit_score = jnp.where(live, row_scores(query_portion, keys) * score_scale, NEG)
        new_big = jnp.maximum(big, jnp.max(logit_score, axis=1))
        weight = jnp.where(live, jnp.exp(logit_score - new_big[:, None]), 0.0)
        fade = jnp.exp(big - new_big)
        total = total * fade + jnp.sum(weight, axis=1)
        acc = acc * fade[:, None] + jnp.dot(
            weight.astype(jnp.bfloat16), values, preferred_element_type=jnp.float32
        )
        return (new_big, total, acc)

    big, total, acc = state
    return lax.map(one, (query_blocks, big, total, acc))


def student_tile(loop_state, block_entry, student_keys, student_values, score_scale):
    key_gradient, squared_terms = loop_state
    query_portion, target = block_entry
    logit_score = row_scores(query_portion, student_keys) * score_scale
    peak = jnp.max(logit_score, axis=1, keepdims=True)
    weight = jnp.exp(logit_score - peak)
    prob = weight / jnp.sum(weight, axis=1, keepdims=True)
    block_prob = prob.astype(jnp.bfloat16)
    student_output = jnp.dot(block_prob, student_values, preferred_element_type=jnp.float32)
    diff = student_output - target.astype(jnp.float32)
    squared_terms = squared_terms + jnp.sum(diff * diff)
    block_difference = diff.astype(jnp.bfloat16)
    prob_gradient = row_scores(block_difference, student_values)
    inner = jnp.sum(prob * prob_gradient, axis=1, keepdims=True)
    dscore = (prob * (prob_gradient - inner) * score_scale).astype(jnp.bfloat16)
    dkeys = lax.dot_general(
        dscore, query_portion, (((0,), (0,)), ((), ())), preferred_element_type=jnp.float32
    )
    dvals = lax.dot_general(
        block_prob, block_difference, (((0,), (0,)), ((), ())), preferred_element_type=jnp.float32
    )
    key_gradient = key_gradient + jnp.concatenate([dkeys, dvals], axis=1)
    return ((key_gradient, squared_terms), None)


def body(
    queries,
    cache_keys,
    cache_values,
    entry,
    visits,
    doc_length,
    slot_params,
    first_moment,
    second_moment,
):
    shards = lax.axis_size("keys")
    me = lax.axis_index("keys")
    tok, heads, block_width = queries.shape
    rows = tok * heads
    block = math.gcd(rows, 512)
    nblocks = rows // block
    score_scale = 1.0 / math.sqrt(block_width)
    length = doc_length[0]
    query_blocks = queries.reshape(nblocks, block, block_width)
    start = entry[0, 0]
    count = visits[0, 0]
    state = (
        jnp.full((nblocks, block), NEG, jnp.float32),
        jnp.zeros((nblocks, block), jnp.float32),
        jnp.zeros((nblocks, block, block_width), jnp.float32),
    )

    def visit(step, keys, values, loop_state):
        held = jnp.remainder(me - step, shards)
        go = jnp.remainder(-step - start, shards) < count
        return lax.cond(
            go,
            lambda column_index: attend(
                column_index, query_blocks, keys, values, held, length, score_scale
            ),
            lambda column_index: column_index,
            loop_state,
        )

    def turn(step, loop_state):
        keys, values, big, total, acc = loop_state
        big, total, acc = visit(step, keys, values, (big, total, acc))
        keys, values = shifted((keys, values), "keys", 1)
        return (keys, values, big, total, acc)

    keys, values, big, total, acc = lax.fori_loop(
        0, shards - 1, turn, (cache_keys, cache_values) + state
    )
    big, total, acc = visit(shards - 1, keys, values, (big, total, acc))
    teacher_block_list = (acc / total[:, :, None]).astype(jnp.bfloat16)
    teacher_out = teacher_block_list.reshape(tok, heads, block_width)
    copies = slot_params.astype(jnp.bfloat16)
    complete_sum = lax.all_gather(copies, ("keys", "qry"), axis=0, tiled=True)
    student_keys = complete_sum[:, :block_width]
    student_values = complete_sum[:, block_width:]
    initial_state = (jnp.zeros(complete_sum.shape, jnp.float32), jnp.zeros((), jnp.float32))
    (grad_terms, squared_terms), ignored_value = lax.scan(
        lambda column_index, loop_index: student_tile(
            column_index, loop_index, student_keys, student_values, score_scale
        ),
        initial_state,
        (query_blocks, teacher_block_list),
    )
    slot_grad = lax.psum_scatter(grad_terms, ("keys", "qry"), scatter_dimension=0, tiled=True)
    squares_all = lax.psum(squared_terms, ("keys", "qry"))
    loss = (squares_all / (rows * shards * lax.axis_size("qry"))).reshape(1)
    new_first = 0.9 * first_moment + 0.1 * slot_grad
    new_second = 0.95 * second_moment + 0.05 * slot_grad * slot_grad
    new_params = slot_params - 0.02 * new_first / (jnp.sqrt(new_second) + 1e-08)
    return (teacher_out, slot_grad, new_params, new_first, new_second, loss)


def solution(mesh):
    return jax.shard_map(
        body,
        mesh=mesh,
        in_specs=(
            P(("grp", "keys", "qry"), None, None),
            P(("grp", "keys"), None),
            P(("grp", "keys"), None),
            P(("grp", "keys"), "qry"),
            P(("grp", "keys"), "qry"),
            P("grp"),
            P(("grp", "keys", "qry"), None),
            P(("grp", "keys", "qry"), None),
            P(("grp", "keys", "qry"), None),
        ),
        out_specs=(
            P(("grp", "keys", "qry"), None, None),
            P(("grp", "keys", "qry"), None),
            P(("grp", "keys", "qry"), None),
            P(("grp", "keys", "qry"), None),
            P(("grp", "keys", "qry"), None),
            P("grp"),
        ),
        check_vma=False,
    )
```

profile of v0, /device:TPU:0, one launch (start us, length us, event | category | flops | bytes accessed | tf_op | source)
XLA Modules:
  0.0 162.5 jit_solution(8857728833277977669)
XLA Ops:
  8.6 0.8 convert_element_type.42
  9.5 38.7 %all_gather.3 = bf16[1024,256]{1,0:T(8,128)(2,1)S(1)} all-gather(bf16[64,256]{1,0:T(8,128)(2,1)S(1)} %convert_element_type.42), channel_id=1, replica_groups=mesh['grp'=2,'keys'=4,'qry'=4] {'keys','qry'}, dimensions={0}, use_global_device_ids=true | all-gather | bytes 557056 | tf_op jit(solution)/shard_map/all_gather | solution.py:121
  48.3 32.7 %while.82 = (s32[]{:T(128)}, bf16[512,128]{1,0:T(8,128)(2,1)S(1)}, bf16[512,128]{1,0:T(8,128)(2,1)S(1)}, f32[2,512]{1,0:T(2,128)S(1)}, f32[2,512]{1,0:T(2,128)S(...) while((s32[]{:T(128)}, bf16[512,128]{1,0:T(8,128)(2,1)S(1)}, ...), condition=%wide.region_7.8_spmd, body=%wide.region_0.7_spmd.sunk | while | flops 136711200 | bytes 6747030 | solution.py:114
  48.3 0.7 copy.55
  49.0 0.6 copy.56
  49.6 1.7 %collective-permute-start.1 = (bf16[512,128]{1,0:T(8,128)(2,1)}, bf16[512,128]{1,0:T(8,128)(2,1)S(1)}, u32[]{:S(2)}, u32[]{:S(2)}) collective-permute-start(bf16[512,128]{1,0:T(8,128)(2,1)} %copy.56), channel_id=1, source_target_pairs={{12,0},{0,4},{4,8},{8,12},{13,1},{1,5},{5,9},{9,13},{14,2},{2,6},{... | collective-permute-start | bytes 393224 | tf_op jit(solution)/shard_map/while/body/eval_jaxpr/ppermute | solution.py:13
  52.6 7.5 %conditional.4 = ((f32[2,512]{1,0:T(2,128)S(1)}, f32[2,512]{1,0:T(2,128)S(1)}, f32[2,512,128]{2,1,0:T(8,128)S(1)})) conditional(s32[]{:T(128)} %convert_element_type.75, (f32[2,512]{1,0:T(2,128)S(1)}, f32[2,512]{1,0:T(2,128)S(1)}, f32[2,512,128]{2,1,0:T(8,128)S(1)}) %tuple.135, (s32[]{:T(128)}, s32[]{:T(128)}, s32[]{:T(128)}, f32[2,512]{1,0:T(2,128)S(1)}, ...), branch_computations={%region_1.1_spmd, %region_2.6_spmd} | conditional | flops 136711184 | bytes 5173698 | solution.py:99
  52.7 7.4 %while.80 = (s32[]{:T(128)}, f32[2,512]{1,0:T(2,128)S(1)}, f32[2,512]{1,0:T(2,128)S(1)}, f32[2,512,128]{2,1,0:T(8,128)S(1)}, f32[2,512]{1,0:T(2,128)S(1)}, /*ind...) while((s32[]{:T(128)}, f32[2,512]{1,0:T(2,128)S(1)}, ...), condition=%wide.region_6.5_spmd.clone, body=%wide.region_3.4_spmd.clone.sunk | while | flops 136711168 | bytes 4108453 | solution.py:40
  52.7 0.7 compare_reduce_fusion.4
  53.4 1.2 fusion.104
  54.6 1.4 fusion.106
  56.4 0.7 compare_reduce_fusion.4
  57.1 1.2 fusion.104
  58.3 1.4 fusion.106
  60.2 0.7 copy.55
  60.8 0.6 copy.56
  61.5 0.6 collective-permute-start.1
  63.4 7.5 %conditional.4 = ((f32[2,512]{1,0:T(2,128)S(1)}, f32[2,512]{1,0:T(2,128)S(1)}, f32[2,512,128]{2,1,0:T(8,128)S(1)})) conditional(s32[]{:T(128)} %convert_element_type.75, (f32[2,512]{1,0:T(2,128)S(1)}, f32[2,512]{1,0:T(2,128)S(1)}, f32[2,512,128]{2,1,0:T(8,128)S(1)}) %tuple.135, (s32[]{:T(128)}, s32[]{:T(128)}, s32[]{:T(128)}, f32[2,512]{1,0:T(2,128)S(1)}, ...), branch_computations={%region_1.1_spmd, %region_2.6_spmd} | conditional | flops 136711184 | bytes 5173698 | solution.py:99
  63.4 7.4 %while.80 = (s32[]{:T(128)}, f32[2,512]{1,0:T(2,128)S(1)}, f32[2,512]{1,0:T(2,128)S(1)}, f32[2,512,128]{2,1,0:T(8,128)S(1)}, f32[2,512]{1,0:T(2,128)S(1)}, /*ind...) while((s32[]{:T(128)}, f32[2,512]{1,0:T(2,128)S(1)}, ...), condition=%wide.region_6.5_spmd.clone, body=%wide.region_3.4_spmd.clone.sunk | while | flops 136711168 | bytes 4108453 | solution.py:40
  63.4 0.7 compare_reduce_fusion.4
  64.1 1.2 fusion.104
  65.4 1.4 fusion.106
  67.1 0.7 compare_reduce_fusion.4
  67.8 1.2 fusion.104
  69.0 1.4 fusion.106
  70.9 0.7 copy.55
  71.6 0.6 copy.56
  73.5 7.5 %conditional.4 = ((f32[2,512]{1,0:T(2,128)S(1)}, f32[2,512]{1,0:T(2,128)S(1)}, f32[2,512,128]{2,1,0:T(8,128)S(1)})) conditional(s32[]{:T(128)} %convert_element_type.75, (f32[2,512]{1,0:T(2,128)S(1)}, f32[2,512]{1,0:T(2,128)S(1)}, f32[2,512,128]{2,1,0:T(8,128)S(1)}) %tuple.135, (s32[]{:T(128)}, s32[]{:T(128)}, s32[]{:T(128)}, f32[2,512]{1,0:T(2,128)S(1)}, ...), branch_computations={%region_1.1_spmd, %region_2.6_spmd} | conditional | flops 136711184 | bytes 5173698 | solution.py:99
  73.6 7.4 %while.80 = (s32[]{:T(128)}, f32[2,512]{1,0:T(2,128)S(1)}, f32[2,512]{1,0:T(2,128)S(1)}, f32[2,512,128]{2,1,0:T(8,128)S(1)}, f32[2,512]{1,0:T(2,128)S(1)}, /*ind...) while((s32[]{:T(128)}, f32[2,512]{1,0:T(2,128)S(1)}, ...), condition=%wide.region_6.5_spmd.clone, body=%wide.region_3.4_spmd.clone.sunk | while | flops 136711168 | bytes 4108453 | solution.py:40
  73.6 0.7 compare_reduce_fusion.4
  74.3 1.2 fusion.104
  75.5 1.4 fusion.106
  77.3 0.7 compare_reduce_fusion.4
  77.9 1.2 fusion.104
  79.2 1.4 fusion.106
  81.0 3.8 %conditional.2 = ((f32[2,512]{1,0:T(2,128)S(1)}, f32[2,512,128]{2,1,0:T(8,128)S(1)})) conditional(s32[]{:T(128)} %convert_element_type.40, (f32[2,512]{1,0:T(2,128)S(1)}, f32[2,512,128]{2,1,0:T(8,128)S(1)}) %tuple.70, (s32[]{:T(128)}, s32[]{:T(128)}, f32[2,512]{1,0:T(2,128)S(1)}, f32[2,512]{1,0:T(2,128)S(1)}, bf16[2,512,128]{2,1,0:T(8,128)(2,1)S(1)}, ...), branch_computations={%region_8.9_spmd, %region_9.14_spmd} | conditional | flops 136711184 | bytes 5159334 | solution.py:99
  81.1 3.7 %while.81 = (s32[]{:T(128)}, f32[2,512]{1,0:T(2,128)S(1)}, f32[2,512,128]{2,1,0:T(8,128)S(1)}, f32[2,512]{1,0:T(2,128)S(1)}, f32[2,512]{1,0:T(2,128)S(1)}, /*ind...) while((s32[]{:T(128)}, f32[2,512]{1,0:T(2,128)S(1)}, ...), condition=%wide.region_13.13_spmd.clone, body=%wide.region_10.12_spmd.clone.sunk | while | flops 136711168 | bytes 4102297 | solution.py:40
  81.1 0.7 compare_reduce_fusion.5
  82.9 0.7 compare_reduce_fusion.5
  85.0 10.0 %while.83 = (s32[]{:T(128)}, f32[1024,256]{0,1:T(8,128)S(1)}, f32[]{:T(128)}, bf16[2,512,128]{2,1,0:T(8,128)(2,1)S(1)}, bf16[1024,128]{1,0:T(8,128)(2,1)S(1)}, /...) while((s32[]{:T(128)}, f32[1024,256]{0,1:T(8,128)S(1)}, ...), condition=%wide.region_19.20_spmd.clone, body=%wide.region_14.19_spmd.clone.sunk | while | flops 680589824 | bytes 26753152 | solution.py:125
  85.6 0.5 fusion.97
  86.6 1.1 multiply_reduce_fusion.7
  90.6 0.5 fusion.97
  91.6 1.1 multiply_reduce_fusion.7
  95.1 1.3 copy.15
  96.4 31.9 %psum.7 = f32[]{:T(128)} all-reduce(f32[]{:T(128)} %get-tuple-element.654), channel_id=1, replica_groups=mesh['grp'=2,'keys'=4,'qry'=4] {'keys','qry'}, use_global_device_ids=true, to_apply=%region_21.22 | all-reduce | flops 1 | bytes 8 | tf_op jit(solution)/shard_map/psum | solution.py:133
  129.0 24.0 %reduce-scatter.2.cloned.1.call-done = f32[64,256]{1,0:T(8,128)} async-done(((f32[1024,256]{1,0:T(8,128)}), f32[64,256]{1,0:T(8,128)}) %reduce-scatter.2.cloned.1.call-update) | async-done | bytes 65552 | tf_op jit(solution)/shard_map/reduce_scatter | solution.py:132
  153.0 1.5 divide_subtract_fusion
  (116 shorter events, 10.2 us)
Async XLA Ops:
  7.2 41.1 %copy-start = (bf16[128,8,128]{2,1,0:T(8,128)(2,1)S(1)}, bf16[128,8,128]{2,1,0:T(8,128)(2,1)}, u32[]{:S(2)}) copy-start(bf16[128,8,128]{2,1,0:T(8,128)(2,1)} %param.21) | copy-start | bytes 786436
  7.2 41.1 %copy-start.1 = (bf16[512,128]{1,0:T(8,128)(2,1)S(1)}, bf16[512,128]{1,0:T(8,128)(2,1)}, u32[]{:S(2)}) copy-start(bf16[512,128]{1,0:T(8,128)(2,1)} %param.22) | copy-start | bytes 393220
  7.2 41.1 %copy-start.2 = (bf16[512,128]{1,0:T(8,128)(2,1)S(1)}, bf16[512,128]{1,0:T(8,128)(2,1)}, u32[]{:S(2)}) copy-start(bf16[512,128]{1,0:T(8,128)(2,1)} %param.23) | copy-start | bytes 393220
  7.2 145.8 %reduce-scatter.2.cloned.1.call-start = ((), (), s32[]{:S(2)}) async-start(), calls=%async_computation.1 | async-start | bytes 1114112 | tf_op jit(solution)/shard_map/reduce_scatter | solution.py:132
  49.0 11.1 %collective-permute-start = (bf16[512,128]{1,0:T(8,128)(2,1)}, bf16[512,128]{1,0:T(8,128)(2,1)S(1)}, u32[]{:S(2)}, u32[]{:S(2)}) collective-permute-start(bf16[512,128]{1,0:T(8,128)(2,1)} %copy.55), channel_id=1, source_target_pairs={{12,0},{0,4},{4,8},{8,12},{13,1},{1,5},{5,9},{9,13},{14,2},{2,6},{... | collective-permute-start | bytes 393224 | tf_op jit(solution)/shard_map/while/body/eval_jaxpr/ppermute | solution.py:13
  49.6 10.5 %collective-permute-start.1 = (bf16[512,128]{1,0:T(8,128)(2,1)}, bf16[512,128]{1,0:T(8,128)(2,1)S(1)}, u32[]{:S(2)}, u32[]{:S(2)}) collective-permute-start(bf16[512,128]{1,0:T(8,128)(2,1)} %copy.56), channel_id=1, source_target_pairs={{12,0},{0,4},{4,8},{8,12},{13,1},{1,5},{5,9},{9,13},{14,2},{2,6},{... | collective-permute-start | bytes 393224 | tf_op jit(solution)/shard_map/while/body/eval_jaxpr/ppermute | solution.py:13
  60.8 10.0 %collective-permute-start = (bf16[512,128]{1,0:T(8,128)(2,1)}, bf16[512,128]{1,0:T(8,128)(2,1)S(1)}, u32[]{:S(2)}, u32[]{:S(2)}) collective-permute-start(bf16[512,128]{1,0:T(8,128)(2,1)} %copy.55), channel_id=1, source_target_pairs={{12,0},{0,4},{4,8},{8,12},{13,1},{1,5},{5,9},{9,13},{14,2},{2,6},{... | collective-permute-start | bytes 393224 | tf_op jit(solution)/shard_map/while/body/eval_jaxpr/ppermute | solution.py:13
  61.5 9.4 %collective-permute-start.1 = (bf16[512,128]{1,0:T(8,128)(2,1)}, bf16[512,128]{1,0:T(8,128)(2,1)S(1)}, u32[]{:S(2)}, u32[]{:S(2)}) collective-permute-start(bf16[512,128]{1,0:T(8,128)(2,1)} %copy.56), channel_id=1, source_target_pairs={{12,0},{0,4},{4,8},{8,12},{13,1},{1,5},{5,9},{9,13},{14,2},{2,6},{... | collective-permute-start | bytes 393224 | tf_op jit(solution)/shard_map/while/body/eval_jaxpr/ppermute | solution.py:13
  71.5 9.5 %collective-permute-start = (bf16[512,128]{1,0:T(8,128)(2,1)}, bf16[512,128]{1,0:T(8,128)(2,1)S(1)}, u32[]{:S(2)}, u32[]{:S(2)}) collective-permute-start(bf16[512,128]{1,0:T(8,128)(2,1)} %copy.55), channel_id=1, source_target_pairs={{12,0},{0,4},{4,8},{8,12},{13,1},{1,5},{5,9},{9,13},{14,2},{2,6},{... | collective-permute-start | bytes 393224 | tf_op jit(solution)/shard_map/while/body/eval_jaxpr/ppermute | solution.py:13
  72.2 8.8 %collective-permute-start.1 = (bf16[512,128]{1,0:T(8,128)(2,1)}, bf16[512,128]{1,0:T(8,128)(2,1)S(1)}, u32[]{:S(2)}, u32[]{:S(2)}) collective-permute-start(bf16[512,128]{1,0:T(8,128)(2,1)} %copy.56), channel_id=1, source_target_pairs={{12,0},{0,4},{4,8},{8,12},{13,1},{1,5},{5,9},{9,13},{14,2},{2,6},{... | collective-permute-start | bytes 393224 | tf_op jit(solution)/shard_map/while/body/eval_jaxpr/ppermute | solution.py:13
  95.0 59.5 %copy-start.3 = (bf16[2,512,128]{2,1,0:T(8,128)(2,1)}, bf16[2,512,128]{2,1,0:T(8,128)(2,1)S(1)}, u32[]{:S(2)}) copy-start(bf16[2,512,128]{2,1,0:T(8,128)(2,1)S(1)} %get-tuple-element.1306) | copy-start | bytes 786436
  95.0 58.0 %copy-start.4 = (f32[64,256]{1,0:T(8,128)S(1)}, f32[64,256]{1,0:T(8,128)}, u32[]{:S(2)}) copy-start(f32[64,256]{1,0:T(8,128)} %param.27) | copy-start | bytes 196612
  95.0 57.9 %copy-start.5 = (f32[64,256]{1,0:T(8,128)S(1)}, f32[64,256]{1,0:T(8,128)}, u32[]{:S(2)}) copy-start(f32[64,256]{1,0:T(8,128)} %param.28) | copy-start | bytes 196612
  95.1 57.9 %copy-start.6 = (f32[64,256]{1,0:T(8,128)S(1)}, f32[64,256]{1,0:T(8,128)}, u32[]{:S(2)}) copy-start(f32[64,256]{1,0:T(8,128)} %param.29) | copy-start | bytes 196612
Sparse Core Ops, SparseCore 0:
  96.5 56.4 reduce-scatter.1
where the time goes:
time: 163 us
  blocking collectives  70.6 us (43%)
  waiting for transfers between devices  24.1 us (15%)
  matrix products  23.3 us (14%)
  between operations  17.3 us (11%)
  other arithmetic  12.6 us (8%)
  loops' own time  6.18 us (4%)
  local copies, waits for them, and re-layouts  6.17 us (4%)
  starting transfers between devices  2.3 us (1%)
    all_gather x1, blocking collectives, body(): complete_sum = lax.all_gather(copies, ('keys', 'qry'), axis=0, tiled=True)  38.7 us
    psum x1, blocking collectives, body(): squares_all = lax.psum(squared_terms, ('keys', 'qry'))  31.9 us
    reduce_scatter x1, waiting for transfers between devices, body(): lax.psum_scatter(grad_terms, ('keys', 'qry'), scatter_dimension=0, tiled=...  24 us
    dot_general x12, matrix products, row_scores(): lax.dot_general(left, right, (((1,), (1,)), ((), ())), preferred_element_...  10.1 us
    dot_general x8, matrix products, one(): jnp.dot(weight.astype(jnp.bfloat16), values, preferred_element_type=jnp.f...  9.39 us
    lt x8, other arithmetic, attend(): live = (place < length)[None, :]  5.37 us
    another operation x1, loops' own time, body(): lax.fori_loop(0, shards - 1, turn, (cache_keys, cache_values) + state)  4.07 us
    another operation x8, local copies, waits for them, and re-layouts  3.92 us
  transfers between devices with their start and end apart: 7, of which 1 were waited for; matrix products, arithmetic and copies ran while one was open for 15% of the time, Pallas kernels for 0%

commit v1 on v0

--- a/solution.py
+++ b/solution.py
@@ -130,7 +130,7 @@
         (query_blocks, teacher_block_list),
     )
     slot_grad = lax.psum_scatter(grad_terms, ("keys", "qry"), scatter_dimension=0, tiled=True)
-    squares_all = lax.psum(squared_terms, ("keys", "qry"))
+    squares_all = jnp.sum(lax.all_gather(squared_terms, ("keys", "qry")), axis=0)
     loss = (squares_all / (rows * shards * lax.axis_size("qry"))).reshape(1)
     new_first = 0.9 * first_moment + 0.1 * slot_grad
     new_second = 0.95 * second_moment + 0.05 * slot_grad * slot_grad

time: 163 us -> 163 us (level)
    psum x1 -> x0, blocking collectives: 31.9 us -> none  [body(): squares_all = lax.psum(squared_terms, ('keys', 'qry'))]
    unnamed x0 -> x1, blocking collectives: none -> 30.9 us
  transfers between devices with their start and end apart: 7 -> 7, of which waited for: 1 -> 1; matrix products, arithmetic and copies ran while one was open for 15% -> 16% of each run, Pallas kernels for 0% -> 0%
where the time goes in v1:
time: 163 us
  blocking collectives  69.6 us (43%)
  matrix products  23.3 us (14%)
  waiting for transfers between devices  23.2 us (14%)
  between operations  17.4 us (11%)
  other arithmetic  13.2 us (8%)
  local copies, waits for them, and re-layouts  7.52 us (5%)
  loops' own time  6.18 us (4%)
  starting transfers between devices  2.3 us (1%)
    all_gather x1, blocking collectives, body(): complete_sum = lax.all_gather(copies, ('keys', 'qry'), axis=0, tiled=True)  38.7 us
    unnamed x1, blocking collectives  30.9 us
    reduce_scatter x1, waiting for transfers between devices, body(): lax.psum_scatter(grad_terms, ('keys', 'qry'), scatter_dimension=0, tiled=...  23.2 us
    dot_general x12, matrix products, row_scores(): lax.dot_general(left, right, (((1,), (1,)), ((), ())), preferred_element_...  10.1 us
    dot_general x8, matrix products, one(): jnp.dot(weight.astype(jnp.bfloat16), values, preferred_element_type=jnp.f...  9.39 us
    lt x8, other arithmetic, attend(): live = (place < length)[None, :]  5.37 us
    another operation x1, loops' own time, body(): lax.fori_loop(0, shards - 1, turn, (cache_keys, cache_values) + state)  4.07 us
    another operation x8, local copies, waits for them, and re-layouts  3.92 us
  transfers between devices with their start and end apart: 7, of which 1 were waited for; matrix products, arithmetic and copies ran while one was open for 16% of the time, Pallas kernels for 0%

profile of v1, /device:TPU:0, one launch (start us, length us, event | category | flops | bytes accessed | tf_op | source)
XLA Modules:
  0.0 162.6 jit_solution(17164529904798180038)
XLA Ops:
  8.6 0.8 convert_element_type.42
  9.5 38.7 %all_gather.9 = bf16[1024,256]{1,0:T(8,128)(2,1)S(1)} all-gather(bf16[64,256]{1,0:T(8,128)(2,1)S(1)} %convert_element_type.42), channel_id=1, replica_groups=mesh['grp'=2,'keys'=4,'qry'=4] {'keys','qry'}, dimensions={0}, use_global_device_ids=true | all-gather | bytes 557056 | tf_op jit(solution)/shard_map/all_gather | solution.py:121
  48.3 32.7 %while.82 = (s32[]{:T(128)}, bf16[512,128]{1,0:T(8,128)(2,1)S(1)}, bf16[512,128]{1,0:T(8,128)(2,1)S(1)}, f32[2,512]{1,0:T(2,128)S(1)}, f32[2,512]{1,0:T(2,128)S(...) while((s32[]{:T(128)}, bf16[512,128]{1,0:T(8,128)(2,1)S(1)}, ...), condition=%wide.region_7.8_spmd, body=%wide.region_0.7_spmd.sunk | while | flops 136711200 | bytes 6747030 | solution.py:114
  48.3 0.7 copy.55
  49.0 0.6 copy.56
  49.6 1.7 %collective-permute-start.1 = (bf16[512,128]{1,0:T(8,128)(2,1)}, bf16[512,128]{1,0:T(8,128)(2,1)S(1)}, u32[]{:S(2)}, u32[]{:S(2)}) collective-permute-start(bf16[512,128]{1,0:T(8,128)(2,1)} %copy.56), channel_id=1, source_target_pairs={{12,0},{0,4},{4,8},{8,12},{13,1},{1,5},{5,9},{9,13},{14,2},{2,6},{... | collective-permute-start | bytes 393224 | tf_op jit(solution)/shard_map/while/body/eval_jaxpr/ppermute | solution.py:13
  52.6 7.5 %conditional.4 = ((f32[2,512]{1,0:T(2,128)S(1)}, f32[2,512]{1,0:T(2,128)S(1)}, f32[2,512,128]{2,1,0:T(8,128)S(1)})) conditional(s32[]{:T(128)} %convert_element_type.75, (f32[2,512]{1,0:T(2,128)S(1)}, f32[2,512]{1,0:T(2,128)S(1)}, f32[2,512,128]{2,1,0:T(8,128)S(1)}) %tuple.135, (s32[]{:T(128)}, s32[]{:T(128)}, s32[]{:T(128)}, f32[2,512]{1,0:T(2,128)S(1)}, ...), branch_computations={%region_1.1_spmd, %region_2.6_spmd} | conditional | flops 136711184 | bytes 5173698 | solution.py:99
  52.7 7.4 %while.80 = (s32[]{:T(128)}, f32[2,512]{1,0:T(2,128)S(1)}, f32[2,512]{1,0:T(2,128)S(1)}, f32[2,512,128]{2,1,0:T(8,128)S(1)}, f32[2,512]{1,0:T(2,128)S(1)}, /*ind...) while((s32[]{:T(128)}, f32[2,512]{1,0:T(2,128)S(1)}, ...), condition=%wide.region_6.5_spmd.clone, body=%wide.region_3.4_spmd.clone.sunk | while | flops 136711168 | bytes 4108453 | solution.py:40
  52.7 0.7 compare_reduce_fusion.4
  53.4 1.2 fusion.104
  54.6 1.4 fusion.106
  56.4 0.7 compare_reduce_fusion.4
  57.1 1.2 fusion.104
  58.3 1.4 fusion.106
  60.2 0.7 copy.55
  60.8 0.6 copy.56
  63.4 7.5 %conditional.4 = ((f32[2,512]{1,0:T(2,128)S(1)}, f32[2,512]{1,0:T(2,128)S(1)}, f32[2,512,128]{2,1,0:T(8,128)S(1)})) conditional(s32[]{:T(128)} %convert_element_type.75, (f32[2,512]{1,0:T(2,128)S(1)}, f32[2,512]{1,0:T(2,128)S(1)}, f32[2,512,128]{2,1,0:T(8,128)S(1)}) %tuple.135, (s32[]{:T(128)}, s32[]{:T(128)}, s32[]{:T(128)}, f32[2,512]{1,0:T(2,128)S(1)}, ...), branch_computations={%region_1.1_spmd, %region_2.6_spmd} | conditional | flops 136711184 | bytes 5173698 | solution.py:99
  63.4 7.4 %while.80 = (s32[]{:T(128)}, f32[2,512]{1,0:T(2,128)S(1)}, f32[2,512]{1,0:T(2,128)S(1)}, f32[2,512,128]{2,1,0:T(8,128)S(1)}, f32[2,512]{1,0:T(2,128)S(1)}, /*ind...) while((s32[]{:T(128)}, f32[2,512]{1,0:T(2,128)S(1)}, ...), condition=%wide.region_6.5_spmd.clone, body=%wide.region_3.4_spmd.clone.sunk | while | flops 136711168 | bytes 4108453 | solution.py:40
  63.4 0.7 compare_reduce_fusion.4
  64.1 1.2 fusion.104
  65.4 1.4 fusion.106
  67.1 0.7 compare_reduce_fusion.4
  67.8 1.2 fusion.104
  69.0 1.4 fusion.106
  70.9 0.7 copy.55
  71.5 0.6 copy.56
  73.5 7.5 %conditional.4 = ((f32[2,512]{1,0:T(2,128)S(1)}, f32[2,512]{1,0:T(2,128)S(1)}, f32[2,512,128]{2,1,0:T(8,128)S(1)})) conditional(s32[]{:T(128)} %convert_element_type.75, (f32[2,512]{1,0:T(2,128)S(1)}, f32[2,512]{1,0:T(2,128)S(1)}, f32[2,512,128]{2,1,0:T(8,128)S(1)}) %tuple.135, (s32[]{:T(128)}, s32[]{:T(128)}, s32[]{:T(128)}, f32[2,512]{1,0:T(2,128)S(1)}, ...), branch_computations={%region_1.1_spmd, %region_2.6_spmd} | conditional | flops 136711184 | bytes 5173698 | solution.py:99
  73.6 7.4 %while.80 = (s32[]{:T(128)}, f32[2,512]{1,0:T(2,128)S(1)}, f32[2,512]{1,0:T(2,128)S(1)}, f32[2,512,128]{2,1,0:T(8,128)S(1)}, f32[2,512]{1,0:T(2,128)S(1)}, /*ind...) while((s32[]{:T(128)}, f32[2,512]{1,0:T(2,128)S(1)}, ...), condition=%wide.region_6.5_spmd.clone, body=%wide.region_3.4_spmd.clone.sunk | while | flops 136711168 | bytes 4108453 | solution.py:40
  73.6 0.7 compare_reduce_fusion.4
  74.3 1.2 fusion.104
  75.5 1.4 fusion.106
  77.3 0.7 compare_reduce_fusion.4
  77.9 1.2 fusion.104
  79.2 1.4 fusion.106
  81.0 3.8 %conditional.2 = ((f32[2,512]{1,0:T(2,128)S(1)}, f32[2,512,128]{2,1,0:T(8,128)S(1)})) conditional(s32[]{:T(128)} %convert_element_type.40, (f32[2,512]{1,0:T(2,128)S(1)}, f32[2,512,128]{2,1,0:T(8,128)S(1)}) %tuple.70, (s32[]{:T(128)}, s32[]{:T(128)}, f32[2,512]{1,0:T(2,128)S(1)}, f32[2,512]{1,0:T(2,128)S(1)}, bf16[2,512,128]{2,1,0:T(8,128)(2,1)S(1)}, ...), branch_computations={%region_8.9_spmd, %region_9.14_spmd} | conditional | flops 136711184 | bytes 5159334 | solution.py:99
  81.1 3.7 %while.81 = (s32[]{:T(128)}, f32[2,512]{1,0:T(2,128)S(1)}, f32[2,512,128]{2,1,0:T(8,128)S(1)}, f32[2,512]{1,0:T(2,128)S(1)}, f32[2,512]{1,0:T(2,128)S(1)}, /*ind...) while((s32[]{:T(128)}, f32[2,512]{1,0:T(2,128)S(1)}, ...), condition=%wide.region_13.13_spmd.clone, body=%wide.region_10.12_spmd.clone.sunk | while | flops 136711168 | bytes 4102297 | solution.py:40
  81.1 0.7 compare_reduce_fusion.5
  82.9 0.7 compare_reduce_fusion.5
  85.0 10.0 %while.83 = (s32[]{:T(128)}, f32[1024,256]{0,1:T(8,128)S(1)}, f32[]{:T(128)}, bf16[2,512,128]{2,1,0:T(8,128)(2,1)S(1)}, bf16[1024,128]{1,0:T(8,128)(2,1)S(1)}, /...) while((s32[]{:T(128)}, f32[1024,256]{0,1:T(8,128)S(1)}, ...), condition=%wide.region_19.20_spmd.clone, body=%wide.region_14.19_spmd.clone.sunk | while | flops 680589824 | bytes 26753152 | solution.py:125
  86.6 1.1 multiply_reduce_fusion.7
  91.6 1.1 multiply_reduce_fusion.7
  95.1 1.3 copy.15
  96.5 0.6 dynamic-slice
  97.0 0.8 dynamic-update-slice
  97.8 30.9 %all-reduce = f32[16]{0:T(128)S(1)} all-reduce(f32[16]{0:T(128)S(1)} %dynamic-update-slice), channel_id=1, replica_groups=mesh['grp'=2,'keys'=4,'qry'=4] {'keys','qry'}, use_global_device_ids=true, to_apply=%add | all-reduce | flops 16 | bytes 128
  128.7 0.6 reduce_sum.58
  129.9 23.2 %reduce-scatter.2.cloned.1.call-done = f32[64,256]{1,0:T(8,128)} async-done(((f32[1024,256]{1,0:T(8,128)}), f32[64,256]{1,0:T(8,128)}) %reduce-scatter.2.cloned.1.call-update) | async-done | bytes 65552 | tf_op jit(solution)/shard_map/reduce_scatter | solution.py:132
  153.1 1.5 divide_subtract_fusion
  (122 shorter events, 11.9 us)
Async XLA Ops:
  7.2 41.1 %copy-start = (bf16[128,8,128]{2,1,0:T(8,128)(2,1)S(1)}, bf16[128,8,128]{2,1,0:T(8,128)(2,1)}, u32[]{:S(2)}) copy-start(bf16[128,8,128]{2,1,0:T(8,128)(2,1)} %param.21) | copy-start | bytes 786436
  7.2 41.1 %copy-start.1 = (bf16[512,128]{1,0:T(8,128)(2,1)S(1)}, bf16[512,128]{1,0:T(8,128)(2,1)}, u32[]{:S(2)}) copy-start(bf16[512,128]{1,0:T(8,128)(2,1)} %param.22) | copy-start | bytes 393220
  7.2 41.1 %copy-start.2 = (bf16[512,128]{1,0:T(8,128)(2,1)S(1)}, bf16[512,128]{1,0:T(8,128)(2,1)}, u32[]{:S(2)}) copy-start(bf16[512,128]{1,0:T(8,128)(2,1)} %param.23) | copy-start | bytes 393220
  7.2 145.9 %reduce-scatter.2.cloned.1.call-start = ((), (), s32[]{:S(2)}) async-start(), calls=%async_computation.1 | async-start | bytes 1114112 | tf_op jit(solution)/shard_map/reduce_scatter | solution.py:132
  49.0 11.1 %collective-permute-start = (bf16[512,128]{1,0:T(8,128)(2,1)}, bf16[512,128]{1,0:T(8,128)(2,1)S(1)}, u32[]{:S(2)}, u32[]{:S(2)}) collective-permute-start(bf16[512,128]{1,0:T(8,128)(2,1)} %copy.55), channel_id=1, source_target_pairs={{12,0},{0,4},{4,8},{8,12},{13,1},{1,5},{5,9},{9,13},{14,2},{2,6},{... | collective-permute-start | bytes 393224 | tf_op jit(solution)/shard_map/while/body/eval_jaxpr/ppermute | solution.py:13
  49.6 10.5 %collective-permute-start.1 = (bf16[512,128]{1,0:T(8,128)(2,1)}, bf16[512,128]{1,0:T(8,128)(2,1)S(1)}, u32[]{:S(2)}, u32[]{:S(2)}) collective-permute-start(bf16[512,128]{1,0:T(8,128)(2,1)} %copy.56), channel_id=1, source_target_pairs={{12,0},{0,4},{4,8},{8,12},{13,1},{1,5},{5,9},{9,13},{14,2},{2,6},{... | collective-permute-start | bytes 393224 | tf_op jit(solution)/shard_map/while/body/eval_jaxpr/ppermute | solution.py:13
  60.8 10.0 %collective-permute-start = (bf16[512,128]{1,0:T(8,128)(2,1)}, bf16[512,128]{1,0:T(8,128)(2,1)S(1)}, u32[]{:S(2)}, u32[]{:S(2)}) collective-permute-start(bf16[512,128]{1,0:T(8,128)(2,1)} %copy.55), channel_id=1, source_target_pairs={{12,0},{0,4},{4,8},{8,12},{13,1},{1,5},{5,9},{9,13},{14,2},{2,6},{... | collective-permute-start | bytes 393224 | tf_op jit(solution)/shard_map/while/body/eval_jaxpr/ppermute | solution.py:13
  61.5 9.4 %collective-permute-start.1 = (bf16[512,128]{1,0:T(8,128)(2,1)}, bf16[512,128]{1,0:T(8,128)(2,1)S(1)}, u32[]{:S(2)}, u32[]{:S(2)}) collective-permute-start(bf16[512,128]{1,0:T(8,128)(2,1)} %copy.56), channel_id=1, source_target_pairs={{12,0},{0,4},{4,8},{8,12},{13,1},{1,5},{5,9},{9,13},{14,2},{2,6},{... | collective-permute-start | bytes 393224 | tf_op jit(solution)/shard_map/while/body/eval_jaxpr/ppermute | solution.py:13
  71.5 9.5 %collective-permute-start = (bf16[512,128]{1,0:T(8,128)(2,1)}, bf16[512,128]{1,0:T(8,128)(2,1)S(1)}, u32[]{:S(2)}, u32[]{:S(2)}) collective-permute-start(bf16[512,128]{1,0:T(8,128)(2,1)} %copy.55), channel_id=1, source_target_pairs={{12,0},{0,4},{4,8},{8,12},{13,1},{1,5},{5,9},{9,13},{14,2},{2,6},{... | collective-permute-start | bytes 393224 | tf_op jit(solution)/shard_map/while/body/eval_jaxpr/ppermute | solution.py:13
  72.2 8.8 %collective-permute-start.1 = (bf16[512,128]{1,0:T(8,128)(2,1)}, bf16[512,128]{1,0:T(8,128)(2,1)S(1)}, u32[]{:S(2)}, u32[]{:S(2)}) collective-permute-start(bf16[512,128]{1,0:T(8,128)(2,1)} %copy.56), channel_id=1, source_target_pairs={{12,0},{0,4},{4,8},{8,12},{13,1},{1,5},{5,9},{9,13},{14,2},{2,6},{... | collective-permute-start | bytes 393224 | tf_op jit(solution)/shard_map/while/body/eval_jaxpr/ppermute | solution.py:13
  95.0 59.6 %copy-start.3 = (bf16[2,512,128]{2,1,0:T(8,128)(2,1)}, bf16[2,512,128]{2,1,0:T(8,128)(2,1)S(1)}, u32[]{:S(2)}) copy-start(bf16[2,512,128]{2,1,0:T(8,128)(2,1)S(1)} %get-tuple-element.1306) | copy-start | bytes 786436
  95.0 1.4 copy-start.7
  95.0 58.0 %copy-start.4 = (f32[64,256]{1,0:T(8,128)S(1)}, f32[64,256]{1,0:T(8,128)}, u32[]{:S(2)}) copy-start(f32[64,256]{1,0:T(8,128)} %param.27) | copy-start | bytes 196612
  95.1 58.0 %copy-start.5 = (f32[64,256]{1,0:T(8,128)S(1)}, f32[64,256]{1,0:T(8,128)}, u32[]{:S(2)}) copy-start(f32[64,256]{1,0:T(8,128)} %param.28) | copy-start | bytes 196612
  95.1 58.0 %copy-start.6 = (f32[64,256]{1,0:T(8,128)S(1)}, f32[64,256]{1,0:T(8,128)}, u32[]{:S(2)}) copy-start(f32[64,256]{1,0:T(8,128)} %param.29) | copy-start | bytes 196612
Sparse Core Ops, SparseCore 0:
  96.6 56.4 reduce-scatter.1
